TPU v7x, 256 devices: a whole 4x4x8 slice. The times are simulated.
256 devices in a mesh: seq: 8 (over y, core), vocab: 32 (over z, x).
Axes of the slice: x: 4, y: 4, z: 8, core: 2. Of those that a mesh axis runs over, the one named last changes fastest.
Arguments:
- hidden: bfloat16 [2, 1024, 5120], P(None, 'seq'), may hold values from -128 to 128
- head_weight: bfloat16 [5120, 77824], P('seq', 'vocab'), may hold values from -1 to 1
- ref_logits: bfloat16 [2, 1024, 77824], P(None, 'seq', 'vocab'), may hold values from -320 to 320
- token_ids: int32 [2, 1024], P(None, 'seq'), may hold values from 0 to 77823
- end_pos: int32 [2], replicated, may hold values from 512 to 1023
- loss_mask: int32 [2, 1024], P(None, 'seq'), may hold values 0 or 1
- scores: float32 [2], replicated, may hold values from -8 to 8
Outputs:
- logit_grad: bfloat16 [2, 1024, 77824], P(None, 'seq', 'vocab')
- hidden_grad: bfloat16 [2, 1024, 5120], P(None, 'seq', 'vocab')
- advantages: float32 [2, 1024], P(None, 'seq')
All inputs are finite; a program needn't handle non-finite values. No bound on the sum of `loss_mask` on one device may be relied on, other than what follows from the above.
Results may differ from a plain program's by a relative error of at most 0.0039.
The roundings to bfloat16 on the way count: a program that leaves them out, or rounds other values in their place, can miss the bound.
Values may be sent and summed in bfloat16 or wider, within the bound.
No kernel may reach another device: no remote copies, remote signals or barrier semaphores. Data moves between devices by JAX's collectives and lax.ppermute only.
A program may use at most 128 MiB of HBM per device.

v0:
```python
import jax
import jax.numpy as jnp
from jax import lax
from jax.sharding import PartitionSpec as P


def from_behind(shard, axis, by):
    devices = lax.axis_size(axis)
    pairs = [(i, i + by) for i in range(devices) if 0 <= i + by < devices]
    return lax.ppermute(shard, axis, pairs)


def per_device(hidden, head_weight, ref_logits, token_ids, end_pos, loss_mask, scores):
    batch, segment, width = hidden.shape
    vocab_dev = head_weight.shape[1]
    seq_start = lax.axis_index("seq") * segment
    vocab_start = lax.axis_index("vocab") * vocab_dev
    whole_head = lax.all_gather(head_weight, "seq", axis=0, tiled=True)
    logits = jnp.dot(
        hidden.reshape(batch * segment, width), whole_head, preferred_element_type=jnp.float32
    ).reshape(batch, segment, vocab_dev)
    refs = ref_logits.astype(jnp.float32)
    local_top = jnp.max(logits, axis=2)
    local_rtop = jnp.max(refs, axis=2)
    top_policy, top_ref = lax.pmax((local_top, local_rtop), "vocab")
    expo = jnp.exp(logits - top_policy[:, :, None])
    total, ref_total, weighted = lax.psum(
        (
            jnp.sum(expo, axis=2),
            jnp.sum(jnp.exp(refs - top_ref[:, :, None]), axis=2),
            jnp.sum(expo * (logits - refs), axis=2),
        ),
        "vocab",
    )
    lse_policy = top_policy + jnp.log(total)
    lse_ref = top_ref + jnp.log(ref_total)
    kl_value = weighted / total - lse_policy + lse_ref
    position = seq_start + lax.broadcasted_iota(jnp.int32, (1, segment), 1)
    live = ((loss_mask == 1) & (position <= end_pos[:, None])).astype(jnp.float32)
    at_end = (position == end_pos[:, None]).astype(jnp.float32)
    reward = -0.01 * kl_value * live + scores[:, None] * at_end
    upper = (
        lax.broadcasted_iota(jnp.int32, (segment, segment), 0)
        >= lax.broadcasted_iota(jnp.int32, (segment, segment), 1)
    ).astype(jnp.float32)
    local_returns = jnp.dot(reward, upper, precision=lax.Precision.HIGHEST)
    totals = jnp.sum(reward, axis=1)
    carried = jnp.zeros_like(totals)
    for _ in range(lax.axis_size("seq") - 1):
        carried = from_behind(totals + carried, "seq", -1)
    returns = local_returns + carried[:, None]
    count, first_moment, second_moment = lax.psum(
        (jnp.sum(live), jnp.sum(live * returns), jnp.sum(live * returns * returns)), "seq"
    )
    count = jnp.maximum(count, 1.0)
    mean = first_moment / count
    var = second_moment / count - mean * mean
    advantages = (returns - mean) / jnp.sqrt(var + 1e-05)
    factor = live * advantages / count
    prob = jnp.exp(logits - lse_policy[:, :, None])
    column = vocab_start + lax.broadcasted_iota(jnp.int32, (1, 1, vocab_dev), 2)
    onehot = (column == token_ids[:, :, None]).astype(jnp.float32)
    logit_grad = (factor[:, :, None] * (prob - onehot)).astype(jnp.bfloat16)
    partial_grad = lax.dot_general(
        logit_grad.reshape(batch * segment, vocab_dev),
        whole_head,
        (((1,), (1,)), ((), ())),
        preferred_element_type=jnp.float32,
    ).reshape(batch, segment, width)
    hidden_grad = lax.psum_scatter(partial_grad, "vocab", scatter_dimension=2, tiled=True).astype(
        jnp.bfloat16
    )
    return (logit_grad, hidden_grad, advantages)


def solution(mesh):
    in_specs = (
        P(None, "seq", None),
        P("seq", "vocab"),
        P(None, "seq", "vocab"),
        P(None, "seq"),
        P(),
        P(None, "seq"),
        P(),
    )
    out_specs = (P(None, "seq", "vocab"), P(None, "seq", "vocab"), P(None, "seq"))
    return jax.shard_map(
        per_device, mesh=mesh, in_specs=in_specs, out_specs=out_specs, check_vma=False
    )
```

profile of v0, /device:TPU:8, one launch (start us, length us, event | category | flops | bytes accessed | tf_op | source)
XLA Modules:
  0.0 593.1 jit_solution(15525419192187923961)
XLA Ops:
  7.2 0.0 copy-start
  7.2 0.0 all-gather.2.cloned.1.call-start
  7.2 0.7 all-gather.2.cloned.1.call-update
  7.9 0.0 reduce-scatter.2.cloned.1.call-start
  8.0 1.5 reduce_max.24
  9.5 124.9 %all-gather.2.cloned.1.call-done = bf16[5120,2432]{1,0:T(8,128)(2,1)} async-done(((bf16[640,2432]{1,0:T(8,128)(2,1)}), bf16[5120,2432]{1,0:T(8,128)(2,1)}) %all-gather.2.cloned.1.call-update) | async-done | bytes 24903696 | tf_op jit(solution)/shard_map/all_gather | solution.py:18
  134.5 0.0 copy-done
  134.5 13.4 %fusion.14 = (f32[2,128]{1,0:T(2,128)S(1)}, f32[2,128,2432]{2,1,0:T(8,128)}) fusion(bf16[2,128,5120]{2,1,0:T(8,128)(2,1)S(1)} %copy-done, bf16[5120,2432]{1,0:T(8,128)(2,1)} %all-gather.2.cloned.1.call-done), kind=kOutput, calls=%fused_computation.28 | convolution fusion | flops 6375964672 | bytes 30016512 | tf_op jit(solution)/shard_map/dot_general | solution.py:19
  147.8 0.0 copy-start.3
  147.8 0.0 copy-start.4
  147.8 0.0 copy-start.5
  147.8 0.0 copy-start.2
  147.8 75.2 %all-reduce.1 = (f32[2,128]{1,0:T(2,128)S(1)}, f32[2,128]{1,0:T(2,128)S(1)}) all-reduce(f32[2,128]{1,0:T(2,128)S(1)} %get-tuple-element.23, bf16[2,128]{1,0:T(2,128)(2,1)S(1)} %reduce_max.24), channel_id=1, replica_groups=mesh['seq'=8,'vocab'=32] {'vocab'}, use_global_device_ids=true, to_apply=%region_1.0 | all-reduce | flops 512 | bytes 3584 | tf_op jit(solution)/shard_map/pmax | solution.py:25
  223.1 3.2 fusion.5
  226.3 69.6 %all-reduce = (f32[2,128]{1,0:T(2,128)S(1)}, f32[2,128]{1,0:T(2,128)S(1)}, f32[2,128]{1,0:T(2,128)S(1)}) all-reduce(f32[2,128]{1,0:T(2,128)S(1)} %get-tuple-element.4, f32[2,128]{1,0:T(2,128)S(1)} %get-tuple-element.5, f32[2,128]{1,0:T(2,128)S(1)} %get-tuple-element.3), channel_id=1, replica_groups=mesh['seq'=8,'vocab'=32] {'vocab'}, use_global_device_ids=true, to_apply=%region_5.0 | all-reduce | flops 768 | bytes 6144 | tf_op jit(solution)/shard_map/psum | solution.py:27
  296.0 0.0 copy-done.3
  296.0 0.0 copy-done.4
  296.0 0.0 copy-done.5
  296.0 0.2 fusion.12
  296.1 1.9 collective-permute-start
  298.1 1.3 collective-permute-done
  299.4 3.6 collective-permute-start.1
  302.9 1.3 collective-permute-done.1
  304.2 3.6 collective-permute-start.2
  307.8 1.3 collective-permute-done.2
  309.1 3.6 collective-permute-start.3
  312.6 1.3 collective-permute-done.3
  313.9 3.6 collective-permute-start.4
  317.5 1.3 collective-permute-done.4
  318.8 3.6 collective-permute-start.5
  322.3 1.3 collective-permute-done.5
  323.6 3.6 collective-permute-start.6
  327.2 1.3 collective-permute-done.6
  328.5 0.8 select_reduce_fusion
  329.2 12.5 %all-reduce.2 = (f32[]{:T(128)}, f32[]{:T(128)}, f32[]{:T(128)}) all-reduce(f32[]{:T(128)} %get-tuple-element.7, f32[]{:T(128)} %get-tuple-element.8, f32[]{:T(128)} %get-tuple-element.6), channel_id=1, replica_groups=mesh['seq'=8,'vocab'=32] {'seq'}, use_global_device_ids=true, to_apply=%region_16.0 | all-reduce | flops 3 | bytes 24 | tf_op jit(solution)/shard_map/psum | solution.py:52
  343.7 0.6 select_divide_fusion
  344.3 0.0 copy-done.2
  344.3 2.5 multiply_convert_fusion
  346.8 0.0 copy-start.1
  346.8 1.0 copy-done.1
  347.9 14.2 %fusion = f32[2,128,5120]{1,2,0:T(8,128)} fusion(bf16[2,128,2432]{2,1,0:T(8,128)(2,1)S(1)} %multiply_convert_fusion, bf16[5120,2432]{1,0:T(8,128)(2,1)} %all-gather.2.cloned.1.call-done), kind=kOutput, calls=%fused_computation | convolution fusion | flops 6375342080 | bytes 31391744 | tf_op jit(solution)/shard_map/dot_general | solution.py:64
  362.0 0.0 reduce-scatter.2.cloned.1.call-update
  362.1 222.7 %reduce-scatter.2.cloned.1.call-done = f32[2,128,160]{1,2,0:T(8,128)} async-done(((f32[2,128,5120]{1,2,0:T(8,128)}), f32[2,128,160]{1,2,0:T(8,128)}) %reduce-scatter.2.cloned.1.call-update) | async-done | bytes 163856 | tf_op jit(solution)/shard_map/reduce_scatter | solution.py:70
  584.7 1.6 convert_element_type.21
  (8 shorter events, 0.0 us)
Async XLA Ops:
  7.2 127.3 %copy-start = (bf16[2,128,5120]{2,1,0:T(8,128)(2,1)S(1)}, bf16[2,128,5120]{2,1,0:T(8,128)(2,1)}, u32[]{:S(2)}) copy-start(bf16[2,128,5120]{2,1,0:T(8,128)(2,1)} %param.7) | copy-start | bytes 7864324
  7.2 127.3 %all-gather.2.cloned.1.call-start = ((), (), s32[]{:S(2)}) async-start(), calls=%async_computation.1 | async-start | bytes 28016640 | tf_op jit(solution)/shard_map/all_gather | solution.py:18
  7.9 576.8 %reduce-scatter.2.cloned.1.call-start = ((), (), s32[]{:S(2)}) async-start(), calls=%async_computation.2 | async-start | bytes 5406720 | tf_op jit(solution)/shard_map/reduce_scatter | solution.py:70
  147.8 148.1 %copy-start.3 = (s32[2,128]{1,0:T(2,128)S(1)}, s32[2,128]{1,0:T(2,128)}, u32[]{:S(2)}) copy-start(s32[2,128]{1,0:T(2,128)} %param.12) | copy-start | bytes 3076
  147.8 148.1 %copy-start.4 = (f32[2]{0:T(128)S(1)}, f32[2]{0:T(128)}, u32[]{:S(2)}) copy-start(f32[2]{0:T(128)} %param.13) | copy-start | bytes 28
  147.8 148.1 %copy-start.5 = (s32[2]{0:T(128)S(1)}, s32[2]{0:T(128)}, u32[]{:S(2)}) copy-start(s32[2]{0:T(128)} %param.11) | copy-start | bytes 28
  147.8 196.5 %copy-start.2 = (s32[2,128]{1,0:T(2,128)S(1)}, s32[2,128]{1,0:T(2,128)}, u32[]{:S(2)}) copy-start(s32[2,128]{1,0:T(2,128)} %param.10) | copy-start | bytes 3076
  296.1 3.2 collective-permute-start
  299.4 4.8 collective-permute-start.1
  304.2 4.8 collective-permute-start.2
  309.1 4.8 collective-permute-start.3
  313.9 4.8 collective-permute-start.4
  318.8 4.8 collective-permute-start.5
  323.6 4.8 collective-permute-start.6
  346.8 1.0 copy-start.1
Sparse Core Ops, SparseCore 0:
  9.8 124.5 all-gather.1
  362.2 222.4 reduce-scatter.1
where the time goes:
time: 594 us; the launch traced here: 593 us
  waiting for transfers between devices  357 us (60%)
  blocking collectives  157 us (26%)
  matrix products  28.3 us (5%)
  starting transfers between devices  23.4 us (4%)
  between operations  16.2 us (3%)
  other arithmetic  9.68 us (2%)
    reduce_scatter x1, waiting for transfers between devices, per_device(): lax.psum_scatter(partial_grad, 'vocab', scatter_dimension=2, tiled=True)  223 us
    all_gather x1, waiting for transfers between devices, per_device(): whole_head = lax.all_gather(head_weight, 'seq', axis=0, tiled=True)  125 us
    pmax x1, blocking collectives, per_device(): top_policy, top_ref = lax.pmax((local_top, local_rtop), 'vocab')  75.2 us
    psum x1, blocking collectives, per_device(): lax.psum((jnp.sum(expo, axis=2), jnp.sum(jnp.exp(refs - top_ref[:, :, Non...  69.6 us
    ppermute x7, starting transfers between devices, from_behind(): return lax.ppermute(shard, axis, pairs)  23.3 us
    dot_general x1, matrix products, per_device(): lax.dot_general(logit_grad.reshape(batch * segment, vocab_dev), whole_hea...  14.2 us
    dot_general x1, matrix products, per_device(): jnp.dot(hidden.reshape(batch * segment, width), whole_head, preferred_ele...  13.4 us
    psum x1, blocking collectives, per_device(): lax.psum((jnp.sum(live), jnp.sum(live * returns), jnp.sum(live * returns...  12.5 us
  transfers between devices with their start and end apart: 9, of which 9 were waited for; matrix products, arithmetic and copies ran while one was open for 0% of the time, Pallas kernels for 0%

commit v1 on v0

--- a/solution.py
+++ b/solution.py
@@ -15,7 +15,9 @@
     vocab_dev = head_weight.shape[1]
     seq_start = lax.axis_index("seq") * segment
     vocab_start = lax.axis_index("vocab") * vocab_dev
-    whole_head = lax.all_gather(head_weight, "seq", axis=0, tiled=True)
+    whole_head = jnp.concatenate(
+        lax.all_to_all(jnp.stack([head_weight] * lax.axis_size("seq")), "seq", 0, 0), axis=0
+    )
     logits = jnp.dot(
         hidden.reshape(batch * segment, width), whole_head, preferred_element_type=jnp.float32
     ).reshape(batch, segment, vocab_dev)

time: 594 us -> 760 us (1.28)
  waiting for transfers between devices: 357 us -> 499 us
  local copies, waits for them, and re-layouts: 1.05 us -> 15.8 us
  starting transfers between devices: 23.4 us -> 31.8 us
    all_to_all x0 -> x1, waiting for transfers between devices: none -> 269 us  [per_device(): lax.all_to_all(jnp.stack([head_weight] * lax.axis_size('seq')), 'seq', 0, 0)]
    all_gather x1 -> x0, waiting for transfers between devices: 125 us -> none  [per_device(): whole_head = lax.all_gather(head_weight, 'seq', axis=0, tiled=True)]
    another operation x0 -> x1, local copies, waits for them, and re-layouts: none -> 14.7 us  [per_device(): jnp.stack([head_weight] * lax.axis_size('seq'))]
    all_to_all x0 -> x1, starting transfers between devices: none -> 8.49 us  [per_device(): lax.all_to_all(jnp.stack([head_weight] * lax.axis_size('seq')), 'seq', 0, 0)]
where the time goes in v1:
time: 760 us; the launch traced here: 759 us
  waiting for transfers between devices  499 us (66%)
  blocking collectives  158 us (21%)
  starting transfers between devices  31.8 us (4%)
  matrix products  28.3 us (4%)
  between operations  16.1 us (2%)
  local copies, waits for them, and re-layouts  15.8 us (2%)
  other arithmetic  9.68 us (1%)
    all_to_all x1, waiting for transfers between devices, per_device(): lax.all_to_all(jnp.stack([head_weight] * lax.axis_size('seq')), 'seq', 0, 0)  269 us
    reduce_scatter x1, waiting for transfers between devices, per_device(): lax.psum_scatter(partial_grad, 'vocab', scatter_dimension=2, tiled=True)  221 us
    pmax x1, blocking collectives, per_device(): top_policy, top_ref = lax.pmax((local_top, local_rtop), 'vocab')  76.1 us
    psum x1, blocking collectives, per_device(): lax.psum((jnp.sum(expo, axis=2), jnp.sum(jnp.exp(refs - top_ref[:, :, Non...  69.6 us
    ppermute x7, starting transfers between devices, from_behind(): return lax.ppermute(shard, axis, pairs)  23.3 us
  transfers between devices with their start and end apart: 9, of which 9 were waited for; matrix products, arithmetic and copies ran while one was open for 0% of the time, Pallas kernels for 0%

profile of v1, /device:TPU:8, one launch (start us, length us, event | category | flops | bytes accessed | tf_op | source)
XLA Modules:
  0.0 758.7 jit_solution(6258219236786466544)
XLA Ops:
  7.2 0.0 copy-start
  7.2 14.7 %stack.2 = bf16[8,640,2432]{2,1,0:T(8,128)(2,1)} broadcast(bf16[640,2432]{1,0:T(8,128)(2,1)} %param.8), dimensions={1,2} | broadcast | bytes 28016640 | tf_op jit(solution)/shard_map/stack | solution.py:19
  21.9 8.5 %all-to-all-start = ((bf16[8,640,2432]{2,1,0:T(8,128)(2,1)}), bf16[8,640,2432]{2,1,0:T(8,128)(2,1)}, u32[]{:S(2)}, u32[]{:S(2)}) async-start(bf16[8,640,2432]{2,1,0:T(8,128)(2,1)} %stack.2), calls=%async_computation | async-start | bytes 49807360 | tf_op jit(solution)/shard_map/all_to_all | solution.py:19
  30.4 0.0 reduce-scatter.2.cloned.1.call-start
  30.4 1.5 reduce_max.24
  31.9 268.7 %all-to-all-done = bf16[8,640,2432]{2,1,0:T(8,128)(2,1)} async-done(((bf16[8,640,2432]{2,1,0:T(8,128)(2,1)}), bf16[8,640,2432]{2,1,0:T(8,128)(2,1)}, u32[]{:S(2)}, u32[]{:S(2)}) %all-to-all-start) | async-done | bytes 24903712 | tf_op jit(solution)/shard_map/all_to_all | solution.py:19
  300.6 0.0 copy-done
  300.6 13.4 %fusion.10 = (f32[2,128]{1,0:T(2,128)S(1)}, f32[2,128,2432]{2,1,0:T(8,128)}) fusion(bf16[2,128,5120]{2,1,0:T(8,128)(2,1)S(1)} %copy-done, bf16[5120,2432,1]{1,0,2:T(8,128)(2,1)} %bitcast.1), kind=kOutput, calls=%fused_computation.24 | convolution fusion | flops 6375964672 | bytes 30016512 | tf_op jit(solution)/shard_map/dot_general | solution.py:21
  314.0 0.0 copy-start.3
  314.0 0.0 copy-start.4
  314.0 0.0 copy-start.5
  314.0 0.0 copy-start.2
  314.0 76.1 %all-reduce.1 = (f32[2,128]{1,0:T(2,128)S(1)}, f32[2,128]{1,0:T(2,128)S(1)}) all-reduce(f32[2,128]{1,0:T(2,128)S(1)} %get-tuple-element.23, bf16[2,128]{1,0:T(2,128)(2,1)S(1)} %reduce_max.24), channel_id=1, replica_groups=mesh['seq'=8,'vocab'=32] {'vocab'}, use_global_device_ids=true, to_apply=%region_1.0 | all-reduce | flops 512 | bytes 3584 | tf_op jit(solution)/shard_map/pmax | solution.py:27
  390.1 3.2 fusion.1
  393.3 69.6 %all-reduce = (f32[2,128]{1,0:T(2,128)S(1)}, f32[2,128]{1,0:T(2,128)S(1)}, f32[2,128]{1,0:T(2,128)S(1)}) all-reduce(f32[2,128]{1,0:T(2,128)S(1)} %get-tuple-element.4, f32[2,128]{1,0:T(2,128)S(1)} %get-tuple-element.5, f32[2,128]{1,0:T(2,128)S(1)} %get-tuple-element.3), channel_id=1, replica_groups=mesh['seq'=8,'vocab'=32] {'vocab'}, use_global_device_ids=true, to_apply=%region_5.0 | all-reduce | flops 768 | bytes 6144 | tf_op jit(solution)/shard_map/psum | solution.py:29
  463.0 0.0 copy-done.3
  463.0 0.0 copy-done.4
  463.0 0.0 copy-done.5
  463.0 0.2 fusion.8
  463.2 1.9 collective-permute-start
  465.1 1.3 collective-permute-done
  466.4 3.6 collective-permute-start.1
  469.9 1.3 collective-permute-done.1
  471.2 3.6 collective-permute-start.2
  474.8 1.3 collective-permute-done.2
  476.1 3.6 collective-permute-start.3
  479.6 1.3 collective-permute-done.3
  480.9 3.6 collective-permute-start.4
  484.5 1.3 collective-permute-done.4
  485.8 3.6 collective-permute-start.5
  489.3 1.3 collective-permute-done.5
  490.6 3.6 collective-permute-start.6
  494.2 1.3 collective-permute-done.6
  495.5 0.8 select_reduce_fusion
  496.2 12.5 %all-reduce.2 = (f32[]{:T(128)}, f32[]{:T(128)}, f32[]{:T(128)}) all-reduce(f32[]{:T(128)} %get-tuple-element.7, f32[]{:T(128)} %get-tuple-element.8, f32[]{:T(128)} %get-tuple-element.6), channel_id=1, replica_groups=mesh['seq'=8,'vocab'=32] {'seq'}, use_global_device_ids=true, to_apply=%region_16.0 | all-reduce | flops 3 | bytes 24 | tf_op jit(solution)/shard_map/psum | solution.py:54
  510.7 0.6 select_divide_fusion
  511.4 0.0 copy-done.2
  511.4 2.5 multiply_convert_fusion
  513.9 0.0 copy-start.1
  513.9 1.0 copy-done.1
  514.9 14.2 %fusion.11 = f32[2,128,5120]{1,2,0:T(8,128)} fusion(bf16[2,128,2432]{2,1,0:T(8,128)(2,1)S(1)} %multiply_convert_fusion, bf16[5120,2432,1]{1,0,2:T(8,128)(2,1)} %bitcast.1), kind=kOutput, calls=%fused_computation.25 | convolution fusion | flops 6375342080 | bytes 31391744 | tf_op jit(solution)/shard_map/dot_general | solution.py:66
  529.1 0.0 reduce-scatter.2.cloned.1.call-update
  529.1 221.2 %reduce-scatter.2.cloned.1.call-done = f32[2,128,160]{1,2,0:T(8,128)} async-done(((f32[2,128,5120]{1,2,0:T(8,128)}), f32[2,128,160]{1,2,0:T(8,128)}) %reduce-scatter.2.cloned.1.call-update) | async-done | bytes 163856 | tf_op jit(solution)/shard_map/reduce_scatter | solution.py:72
  750.3 1.6 convert_element_type.21
  (8 shorter events, 0.0 us)
Async XLA Ops:
  7.2 293.5 %copy-start = (bf16[2,128,5120]{2,1,0:T(8,128)(2,1)S(1)}, bf16[2,128,5120]{2,1,0:T(8,128)(2,1)}, u32[]{:S(2)}) copy-start(bf16[2,128,5120]{2,1,0:T(8,128)(2,1)} %param.7) | copy-start | bytes 7864324
  21.9 278.7 %all-to-all-start = ((bf16[8,640,2432]{2,1,0:T(8,128)(2,1)}), bf16[8,640,2432]{2,1,0:T(8,128)(2,1)}, u32[]{:S(2)}, u32[]{:S(2)}) async-start(bf16[8,640,2432]{2,1,0:T(8,128)(2,1)} %stack.2), calls=%async_computation | async-start | bytes 49807360 | tf_op jit(solution)/shard_map/all_to_all | solution.py:19
  30.4 719.9 %reduce-scatter.2.cloned.1.call-start = ((), (), s32[]{:S(2)}) async-start(), calls=%async_computation.2 | async-start | bytes 5406720 | tf_op jit(solution)/shard_map/reduce_scatter | solution.py:72
  314.0 149.0 %copy-start.3 = (s32[2,128]{1,0:T(2,128)S(1)}, s32[2,128]{1,0:T(2,128)}, u32[]{:S(2)}) copy-start(s32[2,128]{1,0:T(2,128)} %param.12) | copy-start | bytes 3076
  314.0 149.0 %copy-start.4 = (f32[2]{0:T(128)S(1)}, f32[2]{0:T(128)}, u32[]{:S(2)}) copy-start(f32[2]{0:T(128)} %param.13) | copy-start | bytes 28
  314.0 149.0 %copy-start.5 = (s32[2]{0:T(128)S(1)}, s32[2]{0:T(128)}, u32[]{:S(2)}) copy-start(s32[2]{0:T(128)} %param.11) | copy-start | bytes 28
  314.0 197.4 %copy-start.2 = (s32[2,128]{1,0:T(2,128)S(1)}, s32[2,128]{1,0:T(2,128)}, u32[]{:S(2)}) copy-start(s32[2,128]{1,0:T(2,128)} %param.10) | copy-start | bytes 3076
  463.2 3.2 collective-permute-start
  466.4 4.8 collective-permute-start.1
  471.2 4.8 collective-permute-start.2
  476.1 4.8 collective-permute-start.3
  480.9 4.8 collective-permute-start.4
  485.8 4.8 collective-permute-start.5
  490.6 4.8 collective-permute-start.6
  513.9 1.0 copy-start.1
Sparse Core Ops, SparseCore 0:
  529.2 221.0 reduce-scatter.1
